TPU v7x, 512 devices: a whole 4x4x16 slice. The times are simulated.
512 devices in a mesh: seq: 16 (over z), exp: 32 (over y, x, core).
Axes of the slice: x: 4, y: 4, z: 16, core: 2. Of those that a mesh axis runs over, the one named last changes fastest.
Arguments:
- byte_embed: bfloat16 [32, 2048, 1024], P('exp', 'seq'), may hold values from -16 to 16
- score_weight: float32 [1024], replicated, may hold values from -1 to 1
- norm_gain: float32 [1024], replicated, may hold values from 0.25 to 1.75
- router: bfloat16 [1024, 32], replicated, may hold values from -0.1875 to 0.1875
- routes: int32 [32, 512, 2], P('exp', 'seq'), may hold values from 0 to 31, all different within a row; in each aligned block of 32 rows (0 to 31, 32 to 63, ..., all dimensions but the last counted through in order) at most 3 rows name the same one
- expert_in: bfloat16 [32, 1024, 4096], P('exp', None, 'seq'), may hold values from -0.1875 to 0.1875
- expert_out: bfloat16 [32, 4096, 1024], P('exp', 'seq'), may hold values from -0.09375 to 0.09375
- cotangent: bfloat16 [32, 512, 1024], P('exp', 'seq'), may hold values from -6 to 6
Outputs:
- grad_embed: bfloat16 [32, 2048, 1024], P('exp', 'seq')
- grad_in: float32 [32, 1024, 4096], P('exp', None, 'seq')
- grad_out: float32 [32, 4096, 1024], P('exp', 'seq')
Inputs may be any that keep to these rules, and one draw needn't show every extreme that they name: `routes`: among the 32 tokens of one device, at most 3 pairs name the same expert, and some device reaches 3 for some expert. The two experts of a token differ.
All inputs are finite; a program needn't handle non-finite values.
Results may differ from a plain program's by a relative error of at most 0.014.
Values may be sent and summed in bfloat16 or wider, within the bound.
A program may use at most 64 MiB of HBM per device.

v0:
```python
import jax
import jax.numpy as jnp
from jax import lax
from jax.sharding import PartitionSpec as P

SQRT_HALF = 0.7071067811865476
INV_ROOT_TWO_PI = 0.3989422804014327


def front(inputs, norm_gain, score_weight, router, routes):
    batches, length, features = inputs.shape
    highest = lax.Precision.HIGHEST
    quartets = inputs.reshape(batches, length // 4, 4, features)
    pair_means = quartets.reshape(batches, length // 4, 2, 2, features).mean(axis=3)
    quad_mean = quartets.mean(axis=2)
    score_one = jnp.einsum("btqd,d->btq", quartets, score_weight, precision=highest)
    score_two = jnp.repeat(
        jnp.einsum("btpd,d->btp", pair_means, score_weight, precision=highest), 2, axis=2
    )
    score_four = jnp.broadcast_to(
        jnp.einsum("btd,d->bt", quad_mean, score_weight, precision=highest)[:, :, None],
        score_one.shape,
    )
    largest = jnp.maximum(jnp.maximum(score_one, score_two), score_four)
    weight_one = jnp.exp(score_one - largest)
    weight_two = jnp.exp(score_two - largest)
    weight_four = jnp.exp(score_four - largest)
    denominator = weight_one + weight_two + weight_four
    pair_full = jnp.repeat(pair_means, 2, axis=2)
    blended = (
        weight_one[..., None] * quartets
        + weight_two[..., None] * pair_full
        + weight_four[..., None] * quad_mean[:, :, None, :]
    ) / denominator[..., None]
    tokens = blended.mean(axis=2)
    mean_square = jnp.mean(tokens * tokens, axis=-1, keepdims=True)
    normed = tokens * lax.rsqrt(mean_square + 1e-06) * norm_gain
    logits = jnp.einsum("btd,de->bte", normed, router.astype(jnp.float32), precision=highest)
    experts = logits.shape[-1]
    sigmoid_all = 1.0 / (1.0 + jnp.exp(-logits))
    chosen = (routes[..., None] == jnp.arange(experts, dtype=jnp.int32)).astype(jnp.float32)
    picked = jnp.sum(chosen * sigmoid_all[:, :, None, :], axis=-1)
    gate_values = picked / jnp.sum(picked, axis=-1, keepdims=True)
    return (tokens, normed, gate_values)


def deliver(row_stack, gates_in):
    owned_rows, owned_gates = (
        lax.all_to_all(row_stack, "exp", split_axis=1, concat_axis=1, tiled=True),
        lax.all_to_all(gates_in, "exp", split_axis=1, concat_axis=1, tiled=True),
    )
    return (
        lax.all_gather(owned_rows, "seq", axis=1, tiled=True),
        lax.all_gather(owned_gates, "seq", axis=1, tiled=True),
    )


def per_device(
    byte_embed, score_weight, norm_gain, router, routes, expert_in, expert_out, cotangent
):
    experts_all = router.shape[1]
    token_count = routes.shape[1]
    width_model = byte_embed.shape[2]
    capacity = max(2, 3 * token_count // experts_all)
    owners = lax.axis_size("exp")
    slot_count = lax.axis_size("seq") * owners * capacity
    highest = lax.Precision.HIGHEST
    contract_rows = (((0,), (0,)), ((), ()))
    contract_cols = (((1,), (1,)), ((), ()))

    def local_front(values):
        return front(values, norm_gain, score_weight, router, routes)

    (tokens, normed, gate_values), pullback = jax.vjp(local_front, byte_embed.astype(jnp.float32))
    normed_rows = normed[0].astype(jnp.bfloat16)
    route_rows = routes[0]
    onehot = (route_rows[:, :, None] == jnp.arange(experts_all, dtype=jnp.int32)).astype(jnp.int32)
    running = jnp.cumsum(onehot.reshape(2 * token_count, experts_all), axis=0)
    running = running.reshape(token_count, 2, experts_all)
    position = jnp.sum(onehot * (running - 1), axis=2)
    slot_index = route_rows * capacity + position
    matches = (
        slot_index[:, :, None] == jnp.arange(experts_all * capacity, dtype=jnp.int32)
    ).astype(jnp.float32)
    picker = jnp.sum(matches, axis=1).astype(jnp.bfloat16)
    token_buffer = lax.dot_general(
        picker, normed_rows, contract_rows, preferred_element_type=jnp.float32
    )
    cot_buffer = lax.dot_general(
        picker, cotangent[0], contract_rows, preferred_element_type=jnp.float32
    )
    row_buffer = (
        jnp.stack([token_buffer, cot_buffer])
        .astype(jnp.bfloat16)
        .reshape(2, experts_all, capacity, width_model)
    )
    gate_buffer = jnp.einsum("tks,tk->s", matches, gate_values[0], precision=highest)
    gate_buffer = gate_buffer.astype(jnp.bfloat16).reshape(1, experts_all, capacity)
    weight_in = expert_in[0]
    weight_out = expert_out[0]
    both_rows, slot_gates = deliver(row_buffer, gate_buffer)
    token_rows = both_rows[0].reshape(slot_count, width_model)
    cot_rows = both_rows[1].reshape(slot_count, width_model)
    gate_first = slot_gates.reshape(slot_count).astype(jnp.float32)
    preact = jnp.dot(token_rows, weight_in, preferred_element_type=jnp.float32)
    normal_cdf = 0.5 * (1.0 + jax.scipy.special.erf(preact * SQRT_HALF))
    normal_pdf = INV_ROOT_TWO_PI * jnp.exp(-0.5 * preact * preact)
    hidden = preact * normal_cdf
    upstream = lax.dot_general(
        cot_rows, weight_out, contract_cols, preferred_element_type=jnp.float32
    )
    gate_terms = jnp.sum(hidden * upstream, axis=1)
    hidden_grad = (gate_first[:, None] * upstream * (normal_cdf + preact * normal_pdf)).astype(
        jnp.bfloat16
    )
    gated_hidden = (gate_first[:, None] * hidden).astype(jnp.bfloat16)
    grad_out = lax.dot_general(
        gated_hidden, cot_rows, contract_rows, preferred_element_type=jnp.float32
    )
    grad_in = lax.dot_general(
        token_rows, hidden_grad, contract_rows, preferred_element_type=jnp.float32
    )
    own_slots = owners * capacity
    summed_rows = lax.psum_scatter(
        lax.dot_general(
            hidden_grad, weight_in, contract_cols, preferred_element_type=jnp.float32
        ).astype(jnp.bfloat16),
        "seq",
        scatter_dimension=0,
        tiled=True,
    )
    every_term = lax.psum(gate_terms, "seq")
    own_terms = lax.dynamic_slice_in_dim(
        every_term, lax.axis_index("seq") * own_slots, own_slots, 0
    )
    returned_rows, returned_gates = (
        lax.all_to_all(
            summed_rows.reshape(owners, capacity, width_model),
            "exp",
            split_axis=0,
            concat_axis=0,
            tiled=True,
        ),
        lax.all_to_all(
            own_terms.astype(jnp.bfloat16).reshape(owners, capacity),
            "exp",
            split_axis=0,
            concat_axis=0,
            tiled=True,
        ),
    )
    normed_grad = jnp.dot(
        picker,
        returned_rows.reshape(experts_all * capacity, width_model),
        preferred_element_type=jnp.float32,
    )
    gate_grad = jnp.einsum(
        "tks,s->tk", matches, returned_gates.reshape(-1).astype(jnp.float32), precision=highest
    )
    (embed_grad,) = pullback((cotangent.astype(jnp.float32), normed_grad[None], gate_grad[None]))
    return (embed_grad.astype(jnp.bfloat16), grad_in[None], grad_out[None])


def solution(mesh):
    in_specs = (
        P("exp", "seq", None),
        P(),
        P(),
        P(),
        P("exp", "seq", None),
        P("exp", None, "seq"),
        P("exp", "seq", None),
        P("exp", "seq", None),
    )
    out_specs = (P("exp", "seq", None), P("exp", None, "seq"), P("exp", "seq", None))
    return jax.shard_map(
        per_device, mesh=mesh, in_specs=in_specs, out_specs=out_specs, check_vma=False
    )
```

profile of v0, /device:TPU:1, one launch (start us, length us, event | category | flops | bytes accessed | tf_op | source)
XLA Modules:
  0.0 291.5 jit_solution(9137847497761137692)
XLA Ops:
  7.2 1.4 reshape.708
  8.6 1.1 reshape.709
  10.0 0.8 reduce_sum.182
  12.2 0.7 fusion.22
  13.9 1.1 fusion.21
  18.0 20.4 %all_to_all.25 = bf16[2,32,3,1024]{3,0,2,1:T(2,128)(2,1)} all-to-all(bf16[2,32,3,1024]{3,0,2,1:T(2,128)(2,1)S(1)} %copy.132), channel_id=1, replica_groups=mesh['seq'=16,'exp'=32] {'exp'}, dimensions={1} | all-to-all | bytes 786432 | tf_op jit(solution)/shard_map/all_to_all | solution.py:49
  38.5 0.9 add_divide_fusion.1
  40.2 10.5 %all_to_all.26 = bf16[1,32,3]{2,0,1:T(2,128)(2,1)S(1)} all-to-all(bf16[1,32,3]{2,0,1:T(2,128)(2,1)S(1)} %reshape.729), channel_id=1, replica_groups=mesh['seq'=16,'exp'=32] {'exp'}, dimensions={1} | all-to-all | bytes 384 | tf_op jit(solution)/shard_map/all_to_all | solution.py:50
  50.7 33.3 %all_gather.6 = bf16[1,512,3]{2,0,1:T(2,128)(2,1)S(1)} all-gather(bf16[1,32,3]{2,0,1:T(2,128)(2,1)S(1)} %all_to_all.26), channel_id=1, replica_groups=mesh['seq'=16,'exp'=32] {'seq'}, dimensions={1}, use_global_device_ids=true | all-gather | bytes 3264 | tf_op jit(solution)/shard_map/all_gather | solution.py:54
  84.1 0.8 convert_reduce_fusion
  85.0 38.5 %all-gather.2.cloned.1.call-done = bf16[2,512,3,1024]{3,0,2,1:T(2,128)(2,1)} async-done(((bf16[2,32,3,1024]{3,0,2,1:T(2,128)(2,1)}), bf16[2,512,3,1024]{3,0,2,1:T(2,128)(2,1)}) %all-gather.2.cloned.1.call-update) | async-done | bytes 6291472 | tf_op jit(solution)/shard_map/all_gather | solution.py:53
  123.6 34.7 %slice_reduce_fusion = (bf16[512,3,1024]{2,1,0:T(4,128)(2,1)}, bf16[512,3,1024]{2,1,0:T(4,128)(2,1)}) fusion(bf16[2,512,3,1024]{3,0,2,1:T(2,128)(2,1)} %all-gather.2.cloned.1.call-done), kind=kLoop, calls=%fused_computation | loop fusion | bytes 12582912 | tf_op jit(solution)/shard_map/slice | solution.py:102
  158.3 8.8 %reshape_squeeze.6 = bf16[1536,1024]{1,0:T(8,128)(2,1)} reshape(bf16[512,3,1024]{2,1,0:T(4,128)(2,1)} %get-tuple-element.4) | data formatting | bytes 6291456 | tf_op jit(solution)/shard_map/reshape;squeeze | solution.py:103
  167.1 8.9 %reshape_squeeze.7 = bf16[1536,1024]{1,0:T(8,128)(2,1)} reshape(bf16[512,3,1024]{2,1,0:T(4,128)(2,1)} %get-tuple-element.3) | data formatting | bytes 6291456 | tf_op jit(solution)/shard_map/reshape;squeeze | solution.py:102
  176.0 3.0 %fusion.18 = f32[1536,256]{0,1:T(8,128)S(1)} fusion(bf16[1536,1024]{1,0:T(8,128)(2,1)} %reshape_squeeze.6, bf16[1,256,1024]{2,1,0:T(8,128)(2,1)S(1)} %copy-done.50), kind=kOutput, calls=%fused_computation.34 | convolution fusion | flops 805306368 | bytes 5242880 | tf_op jit(solution)/shard_map/dot_general | solution.py:109
  179.1 3.4 %fusion.5 = (bf16[1536,256]{0,1:T(8,128)(2,1)S(1)}, f32[1536]{0:T(1024)}, f32[1536,256]{0,1:T(8,128)}) fusion(f32[1536,256]{0,1:T(8,128)S(1)} %fusion.18, f32[1536]{0:T(1024)S(1)} %reshape.717, bf16[1536,1024]{1,0:T(8,128)(2,1)S(1)} %copy-done.2, bf16[1,1024,256]{2,1,0:T(8,128)(2,1)S(1)} %copy-done), kind=kOutput, calls=%fused_computation.9 | convolution fusion | flops 810809856 | bytes 7614464 | tf_op jit(solution)/shard_map/dot_general | solution.py:105
  182.5 2.7 convolution_convert_fusion
  185.2 0.7 div.162
  185.9 0.7 mul.503
  188.2 0.6 copy.134
  189.5 0.8 copy.135
  190.8 1.0 mul.511
  192.1 24.7 %psum.7 = bf16[1536]{0:T(1024)(128)(2,1)S(1)} all-reduce(f32[1536]{0:T(1024)S(1)} %copy-done.34), channel_id=1, replica_groups=mesh['seq'=16,'exp'=32] {'seq'}, use_global_device_ids=true, to_apply=%region_11.12 | all-reduce | flops 1536 | bytes 9216 | tf_op jit(solution)/shard_map/psum | solution.py:132
  216.9 0.7 all_to_all.20
  217.6 14.2 %all-to-all-start.3 = ((bf16[32,1,3]{2,1,0:T(2,128)(2,1)}), bf16[32,1,3]{2,1,0:T(2,128)(2,1)S(1)}, u32[]{:S(2)}, u32[]{:S(2)}) async-start(bf16[32,1,3]{2,1,0:T(2,128)(2,1)} %all_to_all.20), calls=%async_computation.4 | async-start | bytes 32768 | tf_op jit(solution)/shard_map/all_to_all | solution.py:144
  231.8 4.5 %convolution_bitcast_fusion = f32[1,256,1024]{2,1,0:T(8,128)} fusion(bf16[1536,1024]{1,0:T(8,128)(2,1)} %reshape_squeeze.6, f32[1536]{0:T(1024)S(1)} %copy-done.33, f32[1536,256]{0,1:T(8,128)} %get-tuple-element.27), kind=kOutput, calls=%fused_computation.13 | convolution fusion | flops 807665664 | bytes 5773312 | tf_op jit(solution)/shard_map/dot_general | solution.py:117
  236.4 2.0 convolution_bitcast_fusion.1
  239.3 12.9 %reduce-scatter.2.cloned.1.call-done = bf16[96,1024]{1,0:T(8,128)(2,1)} async-done(((bf16[1536,1024]{1,0:T(8,128)(2,1)}), bf16[96,1024]{1,0:T(8,128)(2,1)}) %reduce-scatter.2.cloned.1.call-update) | async-done | bytes 196624 | tf_op jit(solution)/shard_map/reduce_scatter | solution.py:124
  252.2 1.7 reshape.713
  253.9 16.5 %all-to-all-start.2 = ((bf16[32,3,1024]{2,1,0:T(4,128)(2,1)}), bf16[32,3,1024]{2,1,0:T(4,128)(2,1)S(1)}, u32[]{:S(2)}, u32[]{:S(2)}) async-start(bf16[32,3,1024]{2,1,0:T(4,128)(2,1)} %reshape.713), calls=%async_computation.3 | async-start | bytes 524288 | tf_op jit(solution)/shard_map/all_to_all | solution.py:137
  270.7 8.6 %all-to-all-done.2 = bf16[32,3,1024]{2,1,0:T(4,128)(2,1)S(1)} async-done(((bf16[32,3,1024]{2,1,0:T(4,128)(2,1)}), bf16[32,3,1024]{2,1,0:T(4,128)(2,1)S(1)}, u32[]{:S(2)}, u32[]{:S(2)}) %all-to-all-start.2) | async-done | bytes 196640 | tf_op jit(solution)/shard_map/all_to_all | solution.py:137
  283.9 0.8 convert_element_type.81
  (182 shorter events, 15.0 us)
Async XLA Ops:
  7.2 171.9 %copy-start = (bf16[1,1024,256]{2,1,0:T(8,128)(2,1)S(1)}, bf16[1,1024,256]{2,1,0:T(8,128)(2,1)}, u32[]{:S(2)}) copy-start(bf16[1,1024,256]{2,1,0:T(8,128)(2,1)} %param.13) | copy-start | bytes 1572868
  7.2 116.4 %all-gather.2.cloned.1.call-start = ((), (), s32[]{:S(2)}) async-start(), calls=%async_computation.5 | async-start | bytes 6684672 | tf_op jit(solution)/shard_map/all_gather | solution.py:53
  12.0 3.0 %copy-start.4 = (f32[32,1024]{1,0:T(8,128)}, f32[32,1024]{1,0:T(8,128)S(1)}, u32[]{:S(2)}) copy-start(f32[32,1024]{1,0:T(8,128)S(1)} %broadcast_multiply_fusion.1) | copy-start | bytes 393220
  12.2 2.9 copy-start.35
  13.3 3.3 %copy-start.24 = (f32[1024]{0:T(1024)S(1)}, f32[1024]{0:T(1024)}, u32[]{:S(2)}) copy-start(f32[1024]{0:T(1024)} %param.10) | copy-start | bytes 12292
  13.8 3.5 %copy-start.13 = (bf16[1,32,1024]{2,1,0:T(8,128)(2,1)S(1)}, bf16[1,32,1024]{2,1,0:T(8,128)(2,1)}, u32[]{:S(2)}) copy-start(bf16[1,32,1024]{2,1,0:T(8,128)(2,1)} %param.15) | copy-start | bytes 196612
  13.9 172.0 %copy-start.7 = (f32[32,4]{1,0:T(8,128)}, f32[32,4]{1,0:T(8,128)S(1)}, u32[]{:S(2)}) copy-start(f32[32,4]{1,0:T(8,128)S(1)} %get-tuple-element.20) | copy-start | bytes 1540
  13.9 173.2 %copy-start.9 = (f32[32,4]{1,0:T(8,128)}, f32[32,4]{1,0:T(8,128)S(1)}, u32[]{:S(2)}) copy-start(f32[32,4]{1,0:T(8,128)S(1)} %get-tuple-element.22) | copy-start | bytes 1540
  16.5 23.0 %copy-start.40 = (s32[32,2]{0,1:T(2,128)}, s32[32,2]{0,1:T(2,128)S(1)}, u32[]{:S(2)}) copy-start(s32[32,2]{0,1:T(2,128)S(1)} %multiply_add_fusion.2) | copy-start | bytes 772
  17.1 21.3 %copy-start.11 = (bf16[1024,32]{0,1:T(8,128)(2,1)S(1)}, bf16[1024,32]{0,1:T(8,128)(2,1)}, u32[]{:S(2)}) copy-start(bf16[1024,32]{0,1:T(8,128)(2,1)} %param.11) | copy-start | bytes 196612
  38.4 213.8 %reduce-scatter.2.cloned.1.call-start = ((), (), s32[]{:S(2)}) async-start(), calls=%async_computation.6 | async-start | bytes 3342336 | tf_op jit(solution)/shard_map/reduce_scatter | solution.py:124
  39.5 118.8 %copy-start.28 = (f32[32,2]{0,1:T(2,128)}, f32[32,2]{0,1:T(2,128)S(1)}, u32[]{:S(2)}) copy-start(f32[32,2]{0,1:T(2,128)S(1)} %get-tuple-element.12) | copy-start | bytes 772
  85.0 94.0 %copy-start.32 = (f32[1536]{0:T(1024)}, f32[1536]{0:T(1024)S(1)}, u32[]{:S(2)}) copy-start(f32[1536]{0:T(1024)S(1)} %reshape.717) | copy-start | bytes 18436
  167.1 8.9 %copy-start.50 = (bf16[1,256,1024]{2,1,0:T(8,128)(2,1)S(1)}, bf16[1,256,1024]{2,1,0:T(8,128)(2,1)}, u32[]{:S(2)}) copy-start(bf16[1,256,1024]{2,1,0:T(8,128)(2,1)} %param.14) | copy-start | bytes 1572868
  176.0 3.1 %copy-start.2 = (bf16[1536,1024]{1,0:T(8,128)(2,1)S(1)}, bf16[1536,1024]{1,0:T(8,128)(2,1)}, u32[]{:S(2)}) copy-start(bf16[1536,1024]{1,0:T(8,128)(2,1)} %reshape_squeeze.7) | copy-start | bytes 9437188
  188.2 3.9 %copy-start.38 = (f32[32]{0:T(128)S(1)}, f32[32]{0:T(128)}, u32[]{:S(2)}) copy-start(f32[32]{0:T(128)} %copy-done.37) | copy-start | bytes 388
  188.2 3.9 %copy-start.34 = (f32[1536]{0:T(1024)S(1)}, f32[1536]{0:T(1024)}, u32[]{:S(2)}) copy-start(f32[1536]{0:T(1024)} %get-tuple-element.16) | copy-start | bytes 18436
  188.2 43.6 %copy-start.33 = (f32[1536]{0:T(1024)S(1)}, f32[1536]{0:T(1024)}, u32[]{:S(2)}) copy-start(f32[1536]{0:T(1024)} %copy-done.32) | copy-start | bytes 18436
  217.6 21.1 %all-to-all-start.3 = ((bf16[32,1,3]{2,1,0:T(2,128)(2,1)}), bf16[32,1,3]{2,1,0:T(2,128)(2,1)S(1)}, u32[]{:S(2)}, u32[]{:S(2)}) async-start(bf16[32,1,3]{2,1,0:T(2,128)(2,1)} %all_to_all.20), calls=%async_computation.4 | async-start | bytes 32768 | tf_op jit(solution)/shard_map/all_to_all | solution.py:144
  231.8 4.5 %copy-start.3 = (bf16[1536,1024]{1,0:T(8,128)(2,1)S(1)}, bf16[1536,1024]{1,0:T(8,128)(2,1)}, u32[]{:S(2)}) copy-start(bf16[1536,1024]{1,0:T(8,128)(2,1)} %reshape_squeeze.7) | copy-start | bytes 9437188
  236.3 2.9 copy-start.39
  236.3 2.9 copy-start.27
  236.3 34.1 %copy-start.12 = (bf16[1024,32]{0,1:T(8,128)(2,1)S(1)}, bf16[1024,32]{0,1:T(8,128)(2,1)}, u32[]{:S(2)}) copy-start(bf16[1024,32]{0,1:T(8,128)(2,1)} %param.11) | copy-start | bytes 196612
  236.3 34.1 %copy-start.23 = (f32[32,32]{1,0:T(8,128)S(1)}, f32[32,32]{1,0:T(8,128)}, u32[]{:S(2)}) copy-start(f32[32,32]{1,0:T(8,128)} %get-tuple-element.26) | copy-start | bytes 12292
  238.4 41.1 %copy-start.20 = (bf16[32,96]{1,0:T(8,128)(2,1)S(1)}, bf16[32,96]{1,0:T(8,128)(2,1)}, u32[]{:S(2)}) copy-start(bf16[32,96]{1,0:T(8,128)(2,1)} %copy-done.19) | copy-start | bytes 18436
  238.4 41.1 %copy-start.25 = (f32[1024]{0:T(1024)S(1)}, f32[1024]{0:T(1024)}, u32[]{:S(2)}) copy-start(f32[1024]{0:T(1024)} %param.10) | copy-start | bytes 12292
  238.4 41.5 %copy-start.49 = (f32[32]{0:T(128)S(1)}, f32[32]{0:T(128)}, u32[]{:S(2)}) copy-start(f32[32]{0:T(128)} %copy-done.48) | copy-start | bytes 388
  238.4 41.5 %copy-start.14 = (bf16[1,32,1024]{2,1,0:T(8,128)(2,1)S(1)}, bf16[1,32,1024]{2,1,0:T(8,128)(2,1)}, u32[]{:S(2)}) copy-start(bf16[1,32,1024]{2,1,0:T(8,128)(2,1)} %param.15) | copy-start | bytes 196612
  238.4 41.5 %copy-start.47 = (f32[32]{0:T(128)S(1)}, f32[32]{0:T(128)}, u32[]{:S(2)}) copy-start(f32[32]{0:T(128)} %get-tuple-element.23) | copy-start | bytes 388
  238.4 41.6 %copy-start.5 = (f32[32,1024]{1,0:T(8,128)S(1)}, f32[32,1024]{1,0:T(8,128)}, u32[]{:S(2)}) copy-start(f32[32,1024]{1,0:T(8,128)} %copy-done.4) | copy-start | bytes 393220
  238.4 41.6 %copy-start.10 = (f32[32,4]{1,0:T(8,128)S(1)}, f32[32,4]{1,0:T(8,128)}, u32[]{:S(2)}) copy-start(f32[32,4]{1,0:T(8,128)} %copy-done.9) | copy-start | bytes 1540
  253.9 25.4 %all-to-all-start.2 = ((bf16[32,3,1024]{2,1,0:T(4,128)(2,1)}), bf16[32,3,1024]{2,1,0:T(4,128)(2,1)S(1)}, u32[]{:S(2)}, u32[]{:S(2)}) async-start(bf16[32,3,1024]{2,1,0:T(4,128)(2,1)} %reshape.713), calls=%async_computation.3 | async-start | bytes 524288 | tf_op jit(solution)/shard_map/all_to_all | solution.py:137
  (23 other events, 36.7 us)
Sparse Core Ops, SparseCore 0:
  38.5 85.0 all-gather.1
  185.3 66.7 reduce-scatter.1
where the time goes:
time: 292 us
  blocking collectives  88.9 us (30%)
  local copies, waits for them, and re-layouts  70.2 us (24%)
  waiting for transfers between devices  60.4 us (21%)
  starting transfers between devices  30.8 us (11%)
  matrix products  19.3 us (7%)
  between operations  15 us (5%)
  other arithmetic  6.98 us (2%)
    all_gather x1, waiting for transfers between devices, deliver(): lax.all_gather(owned_rows, 'seq', axis=1, tiled=True)  38.5 us
    slice x1, local copies, waits for them, and re-layouts, per_device(): token_rows = both_rows[0].reshape(slot_count, width_model)  34.7 us
    all_gather x1, blocking collectives, deliver(): lax.all_gather(owned_gates, 'seq', axis=1, tiled=True)  33.3 us
    psum x1, blocking collectives, per_device(): every_term = lax.psum(gate_terms, 'seq')  24.7 us
    all_to_all x1, blocking collectives, deliver(): lax.all_to_all(row_stack, 'exp', split_axis=1, concat_axis=1, tiled=True)  20.4 us
    all_to_all x1, starting transfers between devices, per_device(): lax.all_to_all(summed_rows.reshape(owners, capacity, width_model), 'exp',...  16.5 us
    all_to_all x1, starting transfers between devices, per_device(): lax.all_to_all(own_terms.astype(jnp.bfloat16).reshape(owners, capacity),...  14.2 us
    reduce_scatter x1, waiting for transfers between devices, per_device(): lax.psum_scatter(lax.dot_general(hidden_grad, weight_in, contract_cols, p...  12.9 us
  transfers between devices with their start and end apart: 4, of which 4 were waited for; matrix products, arithmetic and copies ran while one was open for 6% of the time, Pallas kernels for 0%

commit v1 on v0

--- a/solution.py
+++ b/solution.py
@@ -129,7 +129,11 @@
         scatter_dimension=0,
         tiled=True,
     )
-    every_term = lax.psum(gate_terms, "seq")
+    every_term = gate_terms
+    for hop in (1, 2, 4, 8):
+        every_term = every_term + lax.ppermute(
+            every_term, "seq", [(dev, dev ^ hop) for dev in range(16)]
+        )
     own_terms = lax.dynamic_slice_in_dim(
         every_term, lax.axis_index("seq") * own_slots, own_slots, 0
     )

time: 292 us -> 293 us (level)
  blocking collectives: 88.9 us -> 64.4 us
  starting transfers between devices: 30.8 us -> 47 us
  waiting for transfers between devices: 60.4 us -> 65.2 us
  other arithmetic: 6.98 us -> 10.2 us
    psum x1 -> x0, blocking collectives: 24.7 us -> none  [per_device(): every_term = lax.psum(gate_terms, 'seq')]
    ppermute x0 -> x4, starting transfers between devices: none -> 19.2 us  [per_device(): lax.ppermute(every_term, 'seq', [(dev, dev ^ hop) for dev in range(16)])]
    ppermute x0 -> x4, waiting for transfers between devices: none -> 5.89 us  [per_device(): lax.ppermute(every_term, 'seq', [(dev, dev ^ hop) for dev in range(16)])]
    reduce_scatter x1, waiting for transfers between devices: 12.9 us -> 9.1 us  [per_device(): lax.psum_scatter(lax.dot_general(hidden_grad, weight_in, contract_cols, p...]
    all_to_all x1, starting transfers between devices: 14.2 us -> 11.2 us  [per_device(): lax.all_to_all(own_terms.astype(jnp.bfloat16).reshape(owners, capacity),...]
  transfers between devices with their start and end apart: 4 -> 8, of which waited for: 4 -> 7; matrix products, arithmetic and copies ran while one was open for 6% -> 7% of each run, Pallas kernels for 0% -> 0%
where the time goes in v1:
time: 293 us; the launch traced here: 292 us
  local copies, waits for them, and re-layouts  69.8 us (24%)
  waiting for transfers between devices  65.2 us (22%)
  blocking collectives  64.4 us (22%)
  starting transfers between devices  47 us (16%)
  matrix products  20.5 us (7%)
  between operations  14.9 us (5%)
  other arithmetic  10.2 us (3%)
    all_gather x1, waiting for transfers between devices, deliver(): lax.all_gather(owned_rows, 'seq', axis=1, tiled=True)  38.7 us
    slice x1, local copies, waits for them, and re-layouts, per_device(): token_rows = both_rows[0].reshape(slot_count, width_model)  34.7 us
    all_gather x1, blocking collectives, deliver(): lax.all_gather(owned_gates, 'seq', axis=1, tiled=True)  33.5 us
    all_to_all x1, blocking collectives, deliver(): lax.all_to_all(row_stack, 'exp', split_axis=1, concat_axis=1, tiled=True)  20.4 us
    ppermute x4, starting transfers between devices, per_device(): lax.ppermute(every_term, 'seq', [(dev, dev ^ hop) for dev in range(16)])  19.2 us
    all_to_all x1, starting transfers between devices, per_device(): lax.all_to_all(summed_rows.reshape(owners, capacity, width_model), 'exp',...  16.6 us
    all_to_all x1, starting transfers between devices, per_device(): lax.all_to_all(own_terms.astype(jnp.bfloat16).reshape(owners, capacity),...  11.2 us
    all_to_all x1, blocking collectives, deliver(): lax.all_to_all(gates_in, 'exp', split_axis=1, concat_axis=1, tiled=True)  10.5 us
  transfers between devices with their start and end apart: 8, of which 7 were waited for; matrix products, arithmetic and copies ran while one was open for 7% of the time, Pallas kernels for 0%

profile of v1, /device:TPU:1, one launch (start us, length us, event | category | flops | bytes accessed | tf_op | source)
XLA Modules:
  0.0 292.1 jit_solution(10904065505559599057)
XLA Ops:
  7.2 1.4 reshape.708
  8.6 1.1 reshape.709
  13.9 1.1 fusion.21
  18.0 20.4 %all_to_all.25 = bf16[2,32,3,1024]{3,0,2,1:T(2,128)(2,1)} all-to-all(bf16[2,32,3,1024]{3,0,2,1:T(2,128)(2,1)S(1)} %copy.132), channel_id=1, replica_groups=mesh['seq'=16,'exp'=32] {'exp'}, dimensions={1} | all-to-all | bytes 786432 | tf_op jit(solution)/shard_map/all_to_all | solution.py:49
  38.5 0.9 add_divide_fusion.1
  39.9 10.5 %all_to_all.26 = bf16[1,32,3]{2,0,1:T(2,128)(2,1)S(1)} all-to-all(bf16[1,32,3]{2,0,1:T(2,128)(2,1)S(1)} %reshape.729), channel_id=1, replica_groups=mesh['seq'=16,'exp'=32] {'exp'}, dimensions={1} | all-to-all | bytes 384 | tf_op jit(solution)/shard_map/all_to_all | solution.py:50
  50.4 33.5 %all_gather.6 = bf16[1,512,3]{2,0,1:T(2,128)(2,1)S(1)} all-gather(bf16[1,32,3]{2,0,1:T(2,128)(2,1)S(1)} %all_to_all.26), channel_id=1, replica_groups=mesh['seq'=16,'exp'=32] {'seq'}, dimensions={1}, use_global_device_ids=true | all-gather | bytes 3264 | tf_op jit(solution)/shard_map/all_gather | solution.py:54
  84.9 38.7 %all-gather.2.cloned.1.call-done = bf16[2,512,3,1024]{3,0,2,1:T(2,128)(2,1)} async-done(((bf16[2,32,3,1024]{3,0,2,1:T(2,128)(2,1)}), bf16[2,512,3,1024]{3,0,2,1:T(2,128)(2,1)}) %all-gather.2.cloned.1.call-update) | async-done | bytes 6291472 | tf_op jit(solution)/shard_map/all_gather | solution.py:53
  123.6 34.7 %slice_reduce_fusion = (bf16[512,3,1024]{2,1,0:T(4,128)(2,1)}, bf16[512,3,1024]{2,1,0:T(4,128)(2,1)}) fusion(bf16[2,512,3,1024]{3,0,2,1:T(2,128)(2,1)} %all-gather.2.cloned.1.call-done), kind=kLoop, calls=%fused_computation | loop fusion | bytes 12582912 | tf_op jit(solution)/shard_map/slice | solution.py:102
  158.3 8.8 %reshape_squeeze.6 = bf16[1536,1024]{1,0:T(8,128)(2,1)} reshape(bf16[512,3,1024]{2,1,0:T(4,128)(2,1)} %get-tuple-element.4) | data formatting | bytes 6291456 | tf_op jit(solution)/shard_map/reshape;squeeze | solution.py:103
  167.1 8.9 %reshape_squeeze.7 = bf16[1536,1024]{1,0:T(8,128)(2,1)} reshape(bf16[512,3,1024]{2,1,0:T(4,128)(2,1)} %get-tuple-element.3) | data formatting | bytes 6291456 | tf_op jit(solution)/shard_map/reshape;squeeze | solution.py:102
  176.0 3.0 %fusion.18 = f32[1536,256]{0,1:T(8,128)S(1)} fusion(bf16[1536,1024]{1,0:T(8,128)(2,1)} %reshape_squeeze.6, bf16[1,256,1024]{2,1,0:T(8,128)(2,1)S(1)} %copy-done.43), kind=kOutput, calls=%fused_computation.34 | convolution fusion | flops 805306368 | bytes 5242880 | tf_op jit(solution)/shard_map/dot_general | solution.py:109
  179.1 2.8 fusion.5
  181.9 2.7 convolution_convert_fusion
  184.6 1.9 collective-permute-start
  186.5 2.5 collective-permute-done
  189.0 2.4 collective-permute-start.1
  191.4 2.9 collective-permute-done.1
  194.9 6.4 %collective-permute-start.2 = (f32[1536]{0:T(1024)}, f32[1536]{0:T(1024)}, u32[]{:S(2)}, u32[]{:S(2)}) collective-permute-start(f32[1536]{0:T(1024)} %add.109), channel_id=1, source_target_pairs={{0,128},{32,160},{64,192},{96,224},{128,0},{160,32},{192,64},{224,... | collective-permute-start | bytes 18440 | tf_op jit(solution)/shard_map/ppermute | solution.py:134
  206.1 0.8 copy.135
  207.5 1.0 mul.511
  209.5 8.5 %collective-permute-start.3 = (f32[1536]{0:T(1024)S(1)}, f32[1536]{0:T(1024)S(1)}, u32[]{:S(2)}, u32[]{:S(2)}) collective-permute-start(f32[1536]{0:T(1024)S(1)} %add.110), channel_id=1, source_target_pairs={{0,256},{32,288},{64,320},{96,352},{128,384},{160,416},{192,448},{... | collective-permute-start | bytes 18440 | tf_op jit(solution)/shard_map/ppermute | solution.py:134
  218.0 4.4 %convolution_bitcast_fusion = f32[1,256,1024]{2,1,0:T(8,128)} fusion(bf16[1536,1024]{1,0:T(8,128)(2,1)} %reshape_squeeze.6, f32[1536]{0:T(1024)} %copy-done.32, f32[1536,256]{0,1:T(8,128)} %get-tuple-element.27), kind=kOutput, calls=%fused_computation.13 | convolution fusion | flops 807665664 | bytes 5773312 | tf_op jit(solution)/shard_map/dot_general | solution.py:117
  223.7 11.2 %all-to-all-start.3 = ((bf16[32,1,3]{2,1,0:T(2,128)(2,1)}), bf16[32,1,3]{2,1,0:T(2,128)(2,1)S(1)}, u32[]{:S(2)}, u32[]{:S(2)}) async-start(bf16[32,1,3]{2,1,0:T(2,128)(2,1)} %all_to_all.20), calls=%async_computation.4 | async-start | bytes 32768 | tf_op jit(solution)/shard_map/all_to_all | solution.py:148
  235.0 3.9 %convolution_bitcast_fusion.1 = f32[1,1024,256]{2,1,0:T(8,128)} fusion(bf16[1536,1024]{1,0:T(8,128)(2,1)} %reshape_squeeze.7, bf16[1536,256]{0,1:T(8,128)(2,1)S(1)} %get-tuple-element.15), kind=kOutput, calls=%fused_computation.14 | convolution fusion | flops 805306368 | bytes 4980736 | tf_op jit(solution)/shard_map/dot_general | solution.py:120
  239.0 2.9 all-to-all-done.3
  242.4 9.1 %reduce-scatter.2.cloned.1.call-done = bf16[96,1024]{1,0:T(8,128)(2,1)} async-done(((bf16[1536,1024]{1,0:T(8,128)(2,1)}), bf16[96,1024]{1,0:T(8,128)(2,1)}) %reduce-scatter.2.cloned.1.call-update) | async-done | bytes 196624 | tf_op jit(solution)/shard_map/reduce_scatter | solution.py:124
  251.5 1.7 reshape.713
  253.3 16.6 %all-to-all-start.2 = ((bf16[32,3,1024]{2,1,0:T(4,128)(2,1)}), bf16[32,3,1024]{2,1,0:T(4,128)(2,1)S(1)}, u32[]{:S(2)}, u32[]{:S(2)}) async-start(bf16[32,3,1024]{2,1,0:T(4,128)(2,1)} %reshape.713), calls=%async_computation.3 | async-start | bytes 524288 | tf_op jit(solution)/shard_map/all_to_all | solution.py:141
  270.1 8.6 %all-to-all-done.2 = bf16[32,3,1024]{2,1,0:T(4,128)(2,1)S(1)} async-done(((bf16[32,3,1024]{2,1,0:T(4,128)(2,1)}), bf16[32,3,1024]{2,1,0:T(4,128)(2,1)S(1)}, u32[]{:S(2)}, u32[]{:S(2)}) %all-to-all-start.2) | async-done | bytes 196640 | tf_op jit(solution)/shard_map/all_to_all | solution.py:141
  279.4 1.1 multiply_reduce_fusion.2
  280.9 1.1 multiply_reduce_fusion.5
  (178 shorter events, 21.6 us)
Async XLA Ops:
  7.2 171.9 %copy-start = (bf16[1,1024,256]{2,1,0:T(8,128)(2,1)S(1)}, bf16[1,1024,256]{2,1,0:T(8,128)(2,1)}, u32[]{:S(2)}) copy-start(bf16[1,1024,256]{2,1,0:T(8,128)(2,1)} %param.13) | copy-start | bytes 1572868
  7.2 116.4 %all-gather.2.cloned.1.call-start = ((), (), s32[]{:S(2)}) async-start(), calls=%async_computation.5 | async-start | bytes 6684672 | tf_op jit(solution)/shard_map/all_gather | solution.py:53
  13.8 3.5 %copy-start.12 = (bf16[1,32,1024]{2,1,0:T(8,128)(2,1)S(1)}, bf16[1,32,1024]{2,1,0:T(8,128)(2,1)}, u32[]{:S(2)}) copy-start(bf16[1,32,1024]{2,1,0:T(8,128)(2,1)} %param.15) | copy-start | bytes 196612
  13.9 188.6 %copy-start.6 = (f32[32,4]{1,0:T(8,128)}, f32[32,4]{1,0:T(8,128)S(1)}, u32[]{:S(2)}) copy-start(f32[32,4]{1,0:T(8,128)S(1)} %get-tuple-element.20) | copy-start | bytes 1540
  13.9 189.9 %copy-start.8 = (f32[32,4]{1,0:T(8,128)}, f32[32,4]{1,0:T(8,128)S(1)}, u32[]{:S(2)}) copy-start(f32[32,4]{1,0:T(8,128)S(1)} %get-tuple-element.22) | copy-start | bytes 1540
  16.6 23.0 %copy-start.37 = (s32[32,2]{0,1:T(2,128)}, s32[32,2]{0,1:T(2,128)S(1)}, u32[]{:S(2)}) copy-start(s32[32,2]{0,1:T(2,128)S(1)} %multiply_add_fusion.2) | copy-start | bytes 772
  17.2 21.3 %copy-start.10 = (bf16[1024,32]{0,1:T(8,128)(2,1)S(1)}, bf16[1024,32]{0,1:T(8,128)(2,1)}, u32[]{:S(2)}) copy-start(bf16[1024,32]{0,1:T(8,128)(2,1)} %param.11) | copy-start | bytes 196612
  38.4 213.1 %reduce-scatter.2.cloned.1.call-start = ((), (), s32[]{:S(2)}) async-start(), calls=%async_computation.6 | async-start | bytes 3342336 | tf_op jit(solution)/shard_map/reduce_scatter | solution.py:124
  39.6 118.7 %copy-start.28 = (f32[32,2]{0,1:T(2,128)}, f32[32,2]{0,1:T(2,128)S(1)}, u32[]{:S(2)}) copy-start(f32[32,2]{0,1:T(2,128)S(1)} %get-tuple-element.12) | copy-start | bytes 772
  39.6 161.7 %copy-start.35 = (f32[32]{0:T(128)}, f32[32]{0:T(128)S(1)}, u32[]{:S(2)}) copy-start(f32[32]{0:T(128)S(1)} %get-tuple-element.11) | copy-start | bytes 388
  84.9 94.2 %copy-start.32 = (f32[1536]{0:T(1024)}, f32[1536]{0:T(1024)S(1)}, u32[]{:S(2)}) copy-start(f32[1536]{0:T(1024)S(1)} %reshape.717) | copy-start | bytes 18436
  167.1 8.9 %copy-start.43 = (bf16[1,256,1024]{2,1,0:T(8,128)(2,1)S(1)}, bf16[1,256,1024]{2,1,0:T(8,128)(2,1)}, u32[]{:S(2)}) copy-start(bf16[1,256,1024]{2,1,0:T(8,128)(2,1)} %param.14) | copy-start | bytes 1572868
  184.6 4.4 %collective-permute-start = (f32[1536]{0:T(1024)S(1)}, f32[1536]{0:T(1024)S(1)}, u32[]{:S(2)}, u32[]{:S(2)}) collective-permute-start(f32[1536]{0:T(1024)S(1)} %get-tuple-element.16), channel_id=1, source_target_pairs={{0,32},{32,0},{64,96},{96,64},{128,160},{160,128},{192,224},{224,1... | collective-permute-start | bytes 18440 | tf_op jit(solution)/shard_map/ppermute | solution.py:134
  189.0 5.3 %collective-permute-start.1 = (f32[1536]{0:T(1024)S(1)}, f32[1536]{0:T(1024)S(1)}, u32[]{:S(2)}, u32[]{:S(2)}) collective-permute-start(f32[1536]{0:T(1024)S(1)} %add.108), channel_id=1, source_target_pairs={{0,64},{32,96},{64,0},{96,32},{128,192},{160,224},{192,128},{224,1... | collective-permute-start | bytes 18440 | tf_op jit(solution)/shard_map/ppermute | solution.py:134
  194.9 13.9 %collective-permute-start.2 = (f32[1536]{0:T(1024)}, f32[1536]{0:T(1024)}, u32[]{:S(2)}, u32[]{:S(2)}) collective-permute-start(f32[1536]{0:T(1024)} %add.109), channel_id=1, source_target_pairs={{0,128},{32,160},{64,192},{96,224},{128,0},{160,32},{192,64},{224,... | collective-permute-start | bytes 18440 | tf_op jit(solution)/shard_map/ppermute | solution.py:134
  209.5 13.4 %collective-permute-start.3 = (f32[1536]{0:T(1024)S(1)}, f32[1536]{0:T(1024)S(1)}, u32[]{:S(2)}, u32[]{:S(2)}) collective-permute-start(f32[1536]{0:T(1024)S(1)} %add.110), channel_id=1, source_target_pairs={{0,256},{32,288},{64,320},{96,352},{128,384},{160,416},{192,448},{... | collective-permute-start | bytes 18440 | tf_op jit(solution)/shard_map/ppermute | solution.py:134
  223.7 18.2 %all-to-all-start.3 = ((bf16[32,1,3]{2,1,0:T(2,128)(2,1)}), bf16[32,1,3]{2,1,0:T(2,128)(2,1)S(1)}, u32[]{:S(2)}, u32[]{:S(2)}) async-start(bf16[32,1,3]{2,1,0:T(2,128)(2,1)} %all_to_all.20), calls=%async_computation.4 | async-start | bytes 32768 | tf_op jit(solution)/shard_map/all_to_all | solution.py:148
  234.9 7.1 %copy-start.38 = (s32[32,2]{0,1:T(2,128)S(1)}, s32[32,2]{0,1:T(2,128)}, u32[]{:S(2)}) copy-start(s32[32,2]{0,1:T(2,128)} %copy-done.37) | copy-start | bytes 772
  234.9 7.3 %copy-start.29 = (f32[32,2]{0,1:T(2,128)S(1)}, f32[32,2]{0,1:T(2,128)}, u32[]{:S(2)}) copy-start(f32[32,2]{0,1:T(2,128)} %copy-done.28) | copy-start | bytes 772
  234.9 7.3 %copy-start.42 = (f32[32]{0:T(128)S(1)}, f32[32]{0:T(128)}, u32[]{:S(2)}) copy-start(f32[32]{0:T(128)} %multiply_divide_fusion.1) | copy-start | bytes 388
  234.9 7.4 %copy-start.36 = (f32[32]{0:T(128)S(1)}, f32[32]{0:T(128)}, u32[]{:S(2)}) copy-start(f32[32]{0:T(128)} %copy-done.35) | copy-start | bytes 388
  234.9 7.4 %copy-start.27 = (s32[1,32,2]{1,2,0:T(2,128)S(1)}, s32[1,32,2]{1,2,0:T(2,128)}, u32[]{:S(2)}) copy-start(s32[1,32,2]{1,2,0:T(2,128)} %param.12) | copy-start | bytes 772
  234.9 34.9 %copy-start.11 = (bf16[1024,32]{0,1:T(8,128)(2,1)S(1)}, bf16[1024,32]{0,1:T(8,128)(2,1)}, u32[]{:S(2)}) copy-start(bf16[1024,32]{0,1:T(8,128)(2,1)} %param.11) | copy-start | bytes 196612
  235.0 34.9 %copy-start.22 = (f32[32,32]{1,0:T(8,128)S(1)}, f32[32,32]{1,0:T(8,128)}, u32[]{:S(2)}) copy-start(f32[32,32]{1,0:T(8,128)} %get-tuple-element.26) | copy-start | bytes 12292
  238.9 40.0 %copy-start.19 = (bf16[32,96]{1,0:T(8,128)(2,1)S(1)}, bf16[32,96]{1,0:T(8,128)(2,1)}, u32[]{:S(2)}) copy-start(bf16[32,96]{1,0:T(8,128)(2,1)} %copy-done.18) | copy-start | bytes 18436
  238.9 40.0 %copy-start.25 = (f32[1024]{0:T(1024)S(1)}, f32[1024]{0:T(1024)}, u32[]{:S(2)}) copy-start(f32[1024]{0:T(1024)} %param.10) | copy-start | bytes 12292
  238.9 40.3 %copy-start.41 = (f32[32]{0:T(128)S(1)}, f32[32]{0:T(128)}, u32[]{:S(2)}) copy-start(f32[32]{0:T(128)} %copy-done.40) | copy-start | bytes 388
  238.9 40.3 %copy-start.13 = (bf16[1,32,1024]{2,1,0:T(8,128)(2,1)S(1)}, bf16[1,32,1024]{2,1,0:T(8,128)(2,1)}, u32[]{:S(2)}) copy-start(bf16[1,32,1024]{2,1,0:T(8,128)(2,1)} %param.15) | copy-start | bytes 196612
  238.9 40.3 %copy-start.39 = (f32[32]{0:T(128)S(1)}, f32[32]{0:T(128)}, u32[]{:S(2)}) copy-start(f32[32]{0:T(128)} %get-tuple-element.23) | copy-start | bytes 388
  238.9 40.4 %copy-start.4 = (f32[32,1024]{1,0:T(8,128)S(1)}, f32[32,1024]{1,0:T(8,128)}, u32[]{:S(2)}) copy-start(f32[32,1024]{1,0:T(8,128)} %copy-done.3) | copy-start | bytes 393220
  238.9 40.4 %copy-start.9 = (f32[32,4]{1,0:T(8,128)S(1)}, f32[32,4]{1,0:T(8,128)}, u32[]{:S(2)}) copy-start(f32[32,4]{1,0:T(8,128)} %copy-done.8) | copy-start | bytes 1540
  253.3 25.5 %all-to-all-start.2 = ((bf16[32,3,1024]{2,1,0:T(4,128)(2,1)}), bf16[32,3,1024]{2,1,0:T(4,128)(2,1)S(1)}, u32[]{:S(2)}, u32[]{:S(2)}) async-start(bf16[32,3,1024]{2,1,0:T(4,128)(2,1)} %reshape.713), calls=%async_computation.3 | async-start | bytes 524288 | tf_op jit(solution)/shard_map/all_to_all | solution.py:141
  (20 other events, 42.3 us)
Sparse Core Ops, SparseCore 0:
  38.5 84.9 all-gather.1
  184.7 66.7 reduce-scatter.1
